TPU v7x, 32 devices: a whole 2x2x4 slice. The times are simulated.
32 devices in a mesh: dp: 8 (over z, x), head: 4 (over y, core).
Axes of the slice: x: 2, y: 2, z: 4, core: 2. Of those that a mesh axis runs over, the one named last changes fastest.
Arguments:
- tokens: bfloat16 [32, 196, 216], P('dp'), may hold values from -6 to 6
- cotangent: float32 [32, 196, 216], P('dp'), may hold values from -6 to 6
- image_count: int32 [8], P('dp'), may hold values from 1 to 4, as said below
- subnet_heads: int32 [1], replicated, may hold values from 6 to 12
- subnet_width: int32 [1], replicated, may hold values from 432 to 864
- block_slot: int32 [12], replicated, may hold values from 0 to 15, as said below
- master: float32 [16, 54, 864], P('dp', None, 'head'), may hold values from -0.8164966 to 0.8164966
- master_m1: float32 [16, 54, 864], P('dp', None, 'head'), may hold values from -187.82971 to 187.82971
- master_m2: float32 [16, 54, 864], P('dp', None, 'head'), may hold values from 78 to 15680
- norm_params: float32 [4, 216], replicated, may hold values from -0.9 to 1.45
- norm_m1: float32 [4, 216], replicated, may hold values from -265.63132 to 265.63132
- norm_m2: float32 [4, 216], replicated, may hold values from 3920 to 35280
- talk: float32 [2, 12, 12], replicated, may hold values from -0.45 to 1.45
- talk_m1: float32 [2, 12, 12], replicated, may hold values from -831.55756 to 831.55756
- talk_m2: float32 [2, 12, 12], replicated, may hold values from 38416 to 307328
- conv: float32 [9, 864], P(None, 'head'), may hold values from -1 to 1
- conv_m1: float32 [9, 864], P(None, 'head'), may hold values from -108.41586 to 108.41586
- conv_m2: float32 [9, 864], P(None, 'head'), may hold values from 653 to 5226
Outputs:
- output: float32 [32, 196, 216], P('dp')
- token_grad: float32 [32, 196, 216], P('dp')
- new_master: float32 [16, 54, 864], P('dp', None, 'head')
- new_master_m1: float32 [16, 54, 864], P('dp', None, 'head')
- new_master_m2: float32 [16, 54, 864], P('dp', None, 'head')
- master_copy: bfloat16 [16, 54, 864], P('dp', None, 'head')
- new_norm: float32 [4, 216], replicated
- new_norm_m1: float32 [4, 216], replicated
- new_norm_m2: float32 [4, 216], replicated
- new_talk: float32 [2, 12, 12], replicated
- new_talk_m1: float32 [2, 12, 12], replicated
- new_talk_m2: float32 [2, 12, 12], replicated
- new_conv: float32 [9, 864], P(None, 'head')
- new_conv_m1: float32 [9, 864], P(None, 'head')
- new_conv_m2: float32 [9, 864], P(None, 'head')
Inputs may be any that keep to these rules, and one draw needn't show every extreme that they name: `image_count`: image slots at or beyond a dp index's count are padding; some dp index holds exactly 4 images and some exactly 1. `block_slot`: the twelve slots are distinct.
All inputs are finite; a program needn't handle non-finite values.
Results may differ from a plain program's by a relative error of at most 0.012.
The roundings to bfloat16 on the way count: a program that leaves them out, or rounds other values in their place, can miss the bound.
Values may be sent and summed in bfloat16 or wider, within the bound.
No kernel may reach another device: no remote copies, remote signals or barrier semaphores. Data moves between devices by JAX's collectives and lax.ppermute only.
A program may use at most 64 MiB of HBM per device.

v0:
```python
import jax
import jax.numpy as jnp
from jax import lax
from jax.sharding import PartitionSpec as P

HD = 18
SIDE = 14
norm_eps = 1e-05
beta_first = 0.5
beta_second = 0.5
adam_eps = 1e-08
rate_matrix = 0.06
rate_small = 0.2
decay_matrix = 0.05
adam_steps = 3
highest = lax.Precision.HIGHEST


def normalize(values, gain_row, bias_row):
    centred = values - jnp.mean(values, axis=-1, keepdims=True)
    inverse = lax.rsqrt(jnp.mean(centred * centred, axis=-1, keepdims=True) + norm_eps)
    scaled = centred * inverse
    return (scaled, inverse, scaled * gain_row + bias_row)


def normalize_back(grad_normed, scaled, inverse, gain_row):
    grad_scaled = grad_normed * gain_row
    centred_grad = grad_scaled - jnp.mean(grad_scaled, axis=-1, keepdims=True)
    return inverse * (
        centred_grad - scaled * jnp.mean(grad_scaled * scaled, axis=-1, keepdims=True)
    )


def pad_grid(values):
    images, length, channels = values.shape
    return jnp.pad(values.reshape(images, SIDE, SIDE, channels), ((0, 0), (1, 1), (1, 1), (0, 0)))


def shifted(padded, row_off, col_off):
    return padded[:, 1 + row_off : 1 + row_off + SIDE, 1 + col_off : 1 + col_off + SIDE, :]


def conv_grid(hidden, kernel):
    padded = pad_grid(hidden)
    summed = jnp.zeros_like(shifted(padded, 0, 0))
    for tap_index in range(9):
        summed = summed + kernel[tap_index] * shifted(padded, tap_index // 3 - 1, tap_index % 3 - 1)
    return summed.reshape(hidden.shape)


def conv_back(grad_act, hidden, kernel):
    padded_grad = pad_grid(grad_act)
    padded_hidden = pad_grid(hidden)
    grad_grid = shifted(padded_grad, 0, 0)
    grad_hidden = jnp.zeros_like(grad_grid)
    kernel_rows = []
    for tap_index in range(9):
        row_off = tap_index // 3 - 1
        col_off = tap_index % 3 - 1
        grad_hidden = grad_hidden + kernel[tap_index] * shifted(padded_grad, -row_off, -col_off)
        kernel_rows.append(
            jnp.sum(grad_grid * shifted(padded_hidden, row_off, col_off), axis=(0, 1, 2))
        )
    return (grad_hidden.reshape(hidden.shape), jnp.stack(kernel_rows))


def mix_scores(received, talk):
    pre_mixed = jnp.einsum(
        "mn,gnqk->gmqk", talk[0], received.astype(jnp.float32), precision=highest
    )
    softmaxed = jax.nn.softmax(pre_mixed, axis=-1)
    post_mixed = jnp.einsum("jm,gmqk->gjqk", talk[1], softmaxed, precision=highest).astype(
        jnp.bfloat16
    )
    return (softmaxed, post_mixed)


def mix_back(grad_post_all, softmaxed, received, talk):
    grad_soft = jnp.einsum("jm,gjqk->gmqk", talk[1], grad_post_all, precision=highest)
    talk_post = jnp.einsum("gjqk,gmqk->jm", grad_post_all, softmaxed, precision=highest)
    grad_mixed = softmaxed * (grad_soft - jnp.sum(grad_soft * softmaxed, axis=-1, keepdims=True))
    talk_pre = jnp.einsum(
        "gmqk,gnqk->mn", grad_mixed, received.astype(jnp.float32), precision=highest
    )
    grad_scores = jnp.einsum("mn,gmqk->gnqk", talk[0], grad_mixed, precision=highest).astype(
        jnp.bfloat16
    )
    return (grad_scores, talk_pre, talk_post)


def adamw(weights_old, gradient, moment_one, moment_two, step_rate, decay_rate):
    one_new = beta_first * moment_one + (1.0 - beta_first) * gradient
    two_new = beta_second * moment_two + (1.0 - beta_second) * gradient * gradient
    hat_one = one_new / (1.0 - beta_first**adam_steps)
    hat_two = two_new / (1.0 - beta_second**adam_steps)
    weights_new = weights_old - step_rate * (
        hat_one / (jnp.sqrt(hat_two) + adam_eps) + decay_rate * weights_old
    )
    return (weights_new, one_new, two_new)


def local(
    tokens,
    cotangent,
    image_count,
    subnet_heads,
    subnet_width,
    block_slot,
    master,
    master_m1,
    master_m2,
    norm_params,
    norm_m1,
    norm_m2,
    talk,
    talk_m1,
    talk_m2,
    conv,
    conv_m1,
    conv_m2,
):
    slot_count = master.shape[0]
    block_rows = master.shape[1]
    model_width = master.shape[2]
    capacity = tokens.shape[0]
    seq_len = tokens.shape[1]
    head_devices = lax.axis_size("head")
    head_place = lax.axis_index("head")
    per_head = block_rows // HD
    hidden_local = 4 * block_rows
    scale_factor = HD ** (-0.5)
    every_slot = lax.all_gather(master.astype(jnp.bfloat16), "dp", axis=0, tiled=True)
    blocks = jnp.take(every_slot, block_slot, axis=0)
    w_qkv = blocks[0:3].reshape(3 * block_rows, model_width)
    w_out = blocks[3]
    w_in = blocks[4:8].reshape(hidden_local, model_width)
    w_down = blocks[8:12].reshape(hidden_local, model_width)
    image_valid = (jnp.arange(capacity) < image_count[0]).astype(jnp.float32)
    head_keep = (head_place * per_head + jnp.arange(per_head) < subnet_heads[0]).astype(jnp.float32)
    unit_keep = (head_place * hidden_local + jnp.arange(hidden_local) < subnet_width[0]).astype(
        jnp.float32
    )
    token_values = tokens.astype(jnp.float32)
    scaled_one, inverse_one, normed_full = normalize(token_values, norm_params[0], norm_params[1])
    normed_one = normed_full.astype(jnp.bfloat16)
    projected = jnp.einsum(
        "gsd,fd->gsf", normed_one, w_qkv, preferred_element_type=jnp.float32
    ).astype(jnp.bfloat16)
    qkv_heads = projected.reshape(capacity, seq_len, 3, per_head, HD)
    queries = qkv_heads[:, :, 0]
    key_vecs = qkv_heads[:, :, 1]
    value_vecs = qkv_heads[:, :, 2]
    scores = (
        jnp.einsum("gqhe,gkhe->ghqk", queries, key_vecs, preferred_element_type=jnp.float32)
        * scale_factor
    ).astype(jnp.bfloat16)
    received = lax.all_to_all(scores, "head", split_axis=2, concat_axis=1, tiled=True)
    softmaxed, post_mixed = mix_scores(received, talk)
    post_local = lax.all_to_all(post_mixed, "head", split_axis=1, concat_axis=2, tiled=True)
    post_local, softmaxed, received = (post_local, softmaxed, received)
    attended = (
        jnp.einsum("ghqk,gkhe->gqhe", post_local, value_vecs, preferred_element_type=jnp.float32)
        * head_keep[None, None, :, None]
    )
    attended = attended.astype(jnp.bfloat16).reshape(capacity, seq_len, per_head * HD)
    saved = (
        scaled_one,
        inverse_one,
        normed_one,
        queries,
        key_vecs,
        value_vecs,
        received,
        softmaxed,
        post_local,
        attended,
    )
    attended = saved[9]
    attn_part = jnp.einsum("gsf,fd->gsd", attended, w_out, preferred_element_type=jnp.float32)
    middle = token_values + lax.psum(attn_part, "head")
    scaled_two, inverse_two, normed_full_two = normalize(middle, norm_params[2], norm_params[3])
    normed_two = normed_full_two.astype(jnp.bfloat16)
    hidden = jnp.einsum("gsd,ud->gsu", normed_two, w_in, preferred_element_type=jnp.float32)
    activated = conv_grid(hidden, conv)
    sigmoid_act = jax.nn.sigmoid(activated)
    gated = (activated * sigmoid_act * unit_keep).astype(jnp.bfloat16)
    down_part = jnp.einsum("gsu,ud->gsd", gated, w_down, preferred_element_type=jnp.float32)
    output = (
        middle + lax.psum(down_part.astype(jnp.bfloat16), "head").astype(jnp.float32)
    ) * image_valid[:, None, None]
    grad_output = cotangent * image_valid[:, None, None]
    grad_low = grad_output.astype(jnp.bfloat16)
    grad_down = jnp.einsum("gsu,gsd->ud", gated, grad_low, preferred_element_type=jnp.float32)
    grad_gated = (
        jnp.einsum("gsd,ud->gsu", grad_low, w_down, preferred_element_type=jnp.float32) * unit_keep
    )
    grad_act = grad_gated * sigmoid_act * (1.0 + activated * (1.0 - sigmoid_act))
    grad_hidden, grad_kernel = conv_back(grad_act, hidden, conv)
    grad_hidden_low = grad_hidden.astype(jnp.bfloat16)
    grad_in = jnp.einsum(
        "gsu,gsd->ud", grad_hidden_low, normed_two, preferred_element_type=jnp.float32
    )
    grad_two_part = jnp.einsum(
        "gsu,ud->gsd", grad_hidden_low, w_in, preferred_element_type=jnp.float32
    )
    grad_normed_two = lax.psum(grad_two_part, "head")
    grad_middle = grad_output + normalize_back(
        grad_normed_two, scaled_two, inverse_two, norm_params[2]
    )
    (
        scaled_one,
        inverse_one,
        normed_one,
        queries,
        key_vecs,
        value_vecs,
        received,
        softmaxed,
        post_local,
        attended,
    ) = saved
    grad_branch = grad_middle.astype(jnp.bfloat16)
    grad_out_proj = jnp.einsum(
        "gsf,gsd->fd", attended, grad_branch, preferred_element_type=jnp.float32
    )
    grad_attended = jnp.einsum(
        "gsd,fd->gsf", grad_branch, w_out, preferred_element_type=jnp.float32
    ).reshape(capacity, seq_len, per_head, HD)
    grad_att_low = (grad_attended * head_keep[None, None, :, None]).astype(jnp.bfloat16)
    grad_values = jnp.einsum(
        "ghqk,gqhe->gkhe", post_local, grad_att_low, preferred_element_type=jnp.float32
    ).astype(jnp.bfloat16)
    grad_post = jnp.einsum(
        "gqhe,gkhe->ghqk", grad_att_low, value_vecs, preferred_element_type=jnp.float32
    ).astype(jnp.bfloat16)
    grad_post_all = lax.all_to_all(
        grad_post, "head", split_axis=2, concat_axis=1, tiled=True
    ).astype(jnp.float32)
    grad_scores, talk_pre, talk_post = mix_back(grad_post_all, softmaxed, received, talk)
    grad_scores_local = lax.all_to_all(grad_scores, "head", split_axis=1, concat_axis=2, tiled=True)
    grad_queries = (
        jnp.einsum(
            "ghqk,gkhe->gqhe", grad_scores_local, key_vecs, preferred_element_type=jnp.float32
        )
        * scale_factor
    ).astype(jnp.bfloat16)
    grad_keys = (
        jnp.einsum(
            "ghqk,gqhe->gkhe", grad_scores_local, queries, preferred_element_type=jnp.float32
        )
        * scale_factor
    ).astype(jnp.bfloat16)
    grad_proj = jnp.stack([grad_queries, grad_keys, grad_values], axis=2).reshape(
        capacity, seq_len, 3 * block_rows
    )
    grad_qkv_w = jnp.einsum(
        "gsf,gsd->fd", grad_proj, normed_one, preferred_element_type=jnp.float32
    )
    grad_one_part = jnp.einsum("gsf,fd->gsd", grad_proj, w_qkv, preferred_element_type=jnp.float32)
    grad_normed_one = lax.psum(grad_one_part, "head")
    token_grad = grad_middle + normalize_back(
        grad_normed_one, scaled_one, inverse_one, norm_params[0]
    )
    share = (jnp.arange(capacity) % head_devices == head_place).astype(jnp.float32)[:, None, None]
    norm_part = jnp.stack(
        [
            jnp.sum(share * grad_normed_one * scaled_one, axis=(0, 1)),
            jnp.sum(share * grad_normed_one, axis=(0, 1)),
            jnp.sum(share * grad_normed_two * scaled_two, axis=(0, 1)),
            jnp.sum(share * grad_normed_two, axis=(0, 1)),
        ]
    )
    talk_part = jnp.stack([talk_pre, talk_post])
    conv_wide = lax.dynamic_update_slice(
        jnp.zeros((9, hidden_local * head_devices), jnp.float32),
        grad_kernel,
        (0, head_place * hidden_local),
    )
    norm_grad, talk_grad, conv_grad_wide = lax.psum(
        (norm_part, talk_part, conv_wide), ("dp", "head")
    )
    conv_grad = lax.dynamic_slice(conv_grad_wide, (0, head_place * hidden_local), (9, hidden_local))
    block_grads = jnp.concatenate(
        [
            grad_qkv_w.reshape(3, block_rows, model_width),
            grad_out_proj[None],
            grad_in.reshape(4, block_rows, model_width),
            grad_down.reshape(4, block_rows, model_width),
        ],
        axis=0,
    )
    all_slots = slot_count * lax.axis_size("dp")
    spread_grads = (
        jnp.zeros((all_slots, block_rows, model_width), jnp.float32).at[block_slot].set(block_grads)
    )
    slot_grads = lax.psum_scatter(spread_grads, "dp", scatter_dimension=0, tiled=True)
    new_master, new_master_m1, new_master_m2 = adamw(
        master, slot_grads, master_m1, master_m2, rate_matrix, decay_matrix
    )
    new_norm, new_norm_m1, new_norm_m2 = adamw(
        norm_params, norm_grad, norm_m1, norm_m2, rate_small, 0.0
    )
    new_talk, new_talk_m1, new_talk_m2 = adamw(talk, talk_grad, talk_m1, talk_m2, rate_small, 0.0)
    new_conv, new_conv_m1, new_conv_m2 = adamw(
        conv, conv_grad, conv_m1, conv_m2, rate_small, decay_matrix
    )
    return (
        output,
        token_grad,
        new_master,
        new_master_m1,
        new_master_m2,
        new_master.astype(jnp.bfloat16),
        new_norm,
        new_norm_m1,
        new_norm_m2,
        new_talk,
        new_talk_m1,
        new_talk_m2,
        new_conv,
        new_conv_m1,
        new_conv_m2,
    )


def solution(mesh):
    in_specs = (
        P("dp", None, None),
        P("dp", None, None),
        P("dp"),
        P(),
        P(),
        P(),
        P("dp", None, "head"),
        P("dp", None, "head"),
        P("dp", None, "head"),
        P(),
        P(),
        P(),
        P(),
        P(),
        P(),
        P(None, "head"),
        P(None, "head"),
        P(None, "head"),
    )
    out_specs = (
        P("dp", None, None),
        P("dp", None, None),
        P("dp", None, "head"),
        P("dp", None, "head"),
        P("dp", None, "head"),
        P("dp", None, "head"),
        P(),
        P(),
        P(),
        P(),
        P(),
        P(),
        P(None, "head"),
        P(None, "head"),
        P(None, "head"),
    )
    return jax.shard_map(local, mesh=mesh, in_specs=in_specs, out_specs=out_specs, check_vma=False)
```

profile of v0, /device:TPU:0, one launch (start us, length us, event | category | flops | bytes accessed | tf_op | source)
XLA Modules:
  0.0 392.8 jit_solution(17498265783803520196)
XLA Ops:
  13.6 32.9 %all_gather.3 = bf16[16,54,216]{2,1,0:T(8,128)(2,1)S(1)} all-gather(bf16[2,54,216]{2,1,0:T(8,128)(2,1)S(1)} %copy.210), channel_id=1, replica_groups=mesh['dp'=8,'head'=4] {'dp'}, dimensions={0}, use_global_device_ids=true | all-gather | bytes 419904 | tf_op jit(solution)/shard_map/all_gather | solution.py:132
  50.7 3.5 all-to-all-start
  54.3 16.1 %all-to-all-done = bf16[4,3,196,196]{3,0,1,2:T(4,128)(2,1)S(1)} async-done(((bf16[4,3,196,196]{3,0,1,2:T(4,128)(2,1)}), bf16[4,3,196,196]{3,0,1,2:T(4,128)(2,1)S(1)}, u32[]{:S(2)}, u32[]{:S(2)}) %all-to-all-start) | async-done | bytes 922016 | tf_op jit(solution)/shard_map/all_to_all | solution.py:157
  70.7 2.0 bitcast_reduce_fusion
  73.9 3.7 fusion.13
  79.3 3.5 all-to-all-start.1
  85.4 13.5 %all-to-all-done.1 = bf16[4,12,49,196]{3,0,2,1:T(4,128)(2,1)S(1)} async-done(((bf16[4,12,49,196]{3,0,2,1:T(4,128)(2,1)}), bf16[4,12,49,196]{3,0,2,1:T(4,128)(2,1)S(1)}, u32[]{:S(2)}, u32[]{:S(2)}) %all-to-all-start.1) | async-done | bytes 922016 | tf_op jit(solution)/shard_map/all_to_all | solution.py:159
  104.0 33.3 %all-reduce.8.cloned.1.call-done = f32[4,196,216]{2,1,0:T(8,128)} async-done(((f32[4,196,216]{2,1,0:T(8,128)}), f32[4,196,216]{2,1,0:T(8,128)}) %all-reduce.8.cloned.1.call-update) | async-done | bytes 677392 | tf_op jit(solution)/shard_map/psum | solution.py:180
  142.9 1.7 multiply_reduce_fusion
  146.9 2.1 fusion.80
  153.6 2.0 convolution_convert_fusion.3
  156.8 25.2 %all-reduce.12.cloned.1.call-done = f32[4,196,216]{2,1,0:T(8,128)} async-done(((f32[4,196,216]{2,1,0:T(8,128)}), f32[4,196,216]{2,1,0:T(8,128)}) %all-reduce.12.cloned.1.call-update) | async-done | bytes 677392 | tf_op jit(solution)/shard_map/psum | solution.py:206
  182.0 2.4 multiply_reduce_fusion.9
  184.4 32.6 %all-reduce.10.cloned.1.call-done = bf16[4,196,216]{2,1,0:T(8,128)(2,1)} async-done(((bf16[4,196,216]{2,1,0:T(8,128)(2,1)}), bf16[4,196,216]{2,1,0:T(8,128)(2,1)}) %all-reduce.10.cloned.1.call-update) | async-done | bytes 338704 | tf_op jit(solution)/shard_map/psum | solution.py:189
  217.0 2.8 multiply_add_fusion.1
  223.1 4.5 %all-to-all-start.2 = ((bf16[4,3,196,196]{3,0,1,2:T(4,128)(2,1)}), bf16[4,3,196,196]{3,0,1,2:T(4,128)(2,1)}, u32[]{:S(2)}, u32[]{:S(2)}) async-start(bf16[4,3,196,196]{3,0,1,2:T(4,128)(2,1)} %copy.239), calls=%async_computation.2 | async-start | bytes 2408448 | tf_op jit(solution)/shard_map/all_to_all | solution.py:236
  227.6 2.2 convolution_bitcast_fusion.1
  229.8 2.4 convolution_bitcast_fusion
  232.2 2.4 copy.276
  235.7 7.8 %all-to-all-done.2 = bf16[4,3,196,196]{3,0,1,2:T(4,128)(2,1)} async-done(((bf16[4,3,196,196]{3,0,1,2:T(4,128)(2,1)}), bf16[4,3,196,196]{3,0,1,2:T(4,128)(2,1)}, u32[]{:S(2)}, u32[]{:S(2)}) %all-to-all-start.2) | async-done | bytes 922016 | tf_op jit(solution)/shard_map/all_to_all | solution.py:236
  243.6 1.7 copy.241
  245.3 4.7 %fusion = (f32[4,12,49]{1,2,0:T(8,128)S(1)}, f32[4,49,196,12]{2,3,1,0:T(8,128)S(1)}) fusion(f32[4,12,49]{1,2,0:T(8,128)S(1)} %copy-done.30, f32[4,12,49]{1,2,0:T(8,128)S(1)} %copy-done.20, f32[4,49,196,12]{2,3,1,0:T(8,128)} %copy-done, f32[2,12,12]{2,1,0:T(8,128)S(1)} %copy-done.40, bf16[4,12,49,196]{3,0,2,1:T(4,128)(2,1)S(1)} %bitcast.228), kind=kOutput, calls=%fused_computation.4 | convolution fusion | flops 68224464 | bytes 5139136 | tf_op jit(solution)/shard_map/jm,gjqk->gmqk/dot_general | solution.py:79
  250.1 4.7 %fusion.14 = bf16[4,12,49,196]{3,1,2,0:T(8,128)(2,1)S(1)} fusion(f32[4,49,196,12]{2,3,1,0:T(8,128)S(1)} %get-tuple-element.136, f32[4,12,49]{1,2,0:T(8,128)S(1)} %get-tuple-element.135, f32[2,12,12]{2,1,0:T(8,128)S(1)} %copy-done.40, f32[4,49,196,12]{2,3,1,0:T(8,128)S(1)} %copy-done.1, f32[4,12,49]{1,2,0:T(8,128)S(1)} %copy-done.30, ...), kind=kOutput, calls=%fused_computation.24 | convolution fusion | flops 68687808 | bytes 7696768 | tf_op jit(solution)/shard_map/mn,gmqk->gnqk/dot_general | solution.py:85
  256.4 4.3 %all-to-all-start.3 = ((bf16[4,12,49,196]{3,0,2,1:T(4,128)(2,1)}), bf16[4,12,49,196]{3,0,2,1:T(4,128)(2,1)}, u32[]{:S(2)}, u32[]{:S(2)}) async-start(bf16[4,12,49,196]{3,0,2,1:T(4,128)(2,1)} %copy.245), calls=%async_computation.3 | async-start | bytes 2408448 | tf_op jit(solution)/shard_map/all_to_all | solution.py:240
  260.7 5.6 %fusion.27 = f32[1,12,12]{2,1,0:T(8,128)S(1)} fusion(bf16[4,12,49,196]{3,0,2,1:T(4,128)(2,1)S(1)} %bitcast.211, f32[4,49,196,12]{2,3,1,0:T(8,128)} %copy-done.68, f32[4,12,49]{1,2,0:T(8,128)S(1)} %get-tuple-element.135, f32[4,49,196,12]{2,3,1,0:T(8,128)} %copy-done, f32[4,12,49]{1,2,0:T(8,128)S(1)} %copy-done.30, f32[4,12,49]{1,2,0:T(8,128)S(1)} %copy-done.20), kind=kOutput, calls=%fused_computation.50 | convolution fusion | flops 68226816 | bytes 4638720 | tf_op jit(solution)/shard_map/gmqk,gnqk->mn/dot_general | solution.py:82
  266.4 2.8 fusion.32
  269.2 7.7 %all-to-all-done.3 = bf16[4,12,49,196]{3,0,2,1:T(4,128)(2,1)} async-done(((bf16[4,12,49,196]{3,0,2,1:T(4,128)(2,1)}), bf16[4,12,49,196]{3,0,2,1:T(4,128)(2,1)}, u32[]{:S(2)}, u32[]{:S(2)}) %all-to-all-start.3) | async-done | bytes 922016 | tf_op jit(solution)/shard_map/all_to_all | solution.py:240
  276.9 1.7 copy.246
  284.2 31.7 %all-reduce.14.cloned.1.call-done = f32[4,196,216]{2,1,0:T(8,128)} async-done(((f32[4,196,216]{2,1,0:T(8,128)}), f32[4,196,216]{2,1,0:T(8,128)}) %all-reduce.14.cloned.1.call-update) | async-done | bytes 677392 | tf_op jit(solution)/shard_map/psum | solution.py:260
  315.9 1.8 fusion.68
  320.7 41.0 %all-reduce.2 = (f32[4,216]{1,0:T(4,128)S(1)}, f32[2,12,12]{2,1,0:T(8,128)S(1)}, f32[9,864]{1,0:T(8,128)S(1)}) all-reduce(f32[4,216]{1,0:T(4,128)S(1)} %pad_maximum_fusion.3, f32[2,12,12]{2,1,0:T(8,128)S(1)} %pad_maximum_fusion.2, f32[9,864]{1,0:T(8,128)S(1)} %copy-done.27), channel_id=1, replica_groups=mesh['dp'=8,'head'=4] {'dp','head'}, use_global_device_ids=true, to_apply=%region_21.22 | all-reduce | flops 8928 | bytes 71424 | tf_op jit(solution)/shard_map/psum | solution.py:279
  364.9 17.6 %reduce-scatter.2.cloned.1.call-done = f32[2,54,216]{2,1,0:T(8,128)} async-done(((f32[16,54,216]{2,1,0:T(8,128)}), f32[2,54,216]{2,1,0:T(8,128)}) %reduce-scatter.2.cloned.1.call-update) | async-done | bytes 93328 | tf_op jit(solution)/shard_map/reduce_scatter | solution.py:296
  (241 shorter events, 53.9 us)
Async XLA Ops:
  7.2 40.6 %copy-start.3 = (bf16[4,196,216]{2,0,1:T(4,128)(2,1)S(1)}, bf16[4,196,216]{2,0,1:T(4,128)(2,1)}, u32[]{:S(2)}) copy-start(bf16[4,196,216]{2,0,1:T(4,128)(2,1)} %param.18) | copy-start | bytes 1016068
  48.6 50.8 %copy-start.17 = (bf16[4,196,1,3,18]{1,0,4,3,2:T(4,128)(2,1)}, bf16[4,196,1,3,18]{1,0,4,3,2:T(4,128)(2,1)S(1)}, u32[]{:S(2)}) copy-start(bf16[4,196,1,3,18]{1,0,4,3,2:T(4,128)(2,1)S(1)} %get-tuple-element.117) | copy-start | bytes 254020
  50.7 19.6 %all-to-all-start = ((bf16[4,3,196,196]{3,0,1,2:T(4,128)(2,1)}), bf16[4,3,196,196]{3,0,1,2:T(4,128)(2,1)S(1)}, u32[]{:S(2)}, u32[]{:S(2)}) async-start(bf16[4,3,196,196]{3,0,1,2:T(4,128)(2,1)} %copy.215), calls=%async_computation | async-start | bytes 2408448 | tf_op jit(solution)/shard_map/all_to_all | solution.py:157
  79.3 19.6 %all-to-all-start.1 = ((bf16[4,12,49,196]{3,0,2,1:T(4,128)(2,1)}), bf16[4,12,49,196]{3,0,2,1:T(4,128)(2,1)S(1)}, u32[]{:S(2)}, u32[]{:S(2)}) async-start(bf16[4,12,49,196]{3,0,2,1:T(4,128)(2,1)} %copy.221), calls=%async_computation.1 | async-start | bytes 2408448 | tf_op jit(solution)/shard_map/all_to_all | solution.py:159
  82.9 54.4 %all-reduce.8.cloned.1.call-start = ((), (), s32[]{:S(2)}) async-start(), calls=%async_computation.5 | async-start | bytes 1638400 | tf_op jit(solution)/shard_map/psum | solution.py:180
  100.9 38.2 %copy-start.44 = (f32[1,216]{1,0:T(1,128)S(1)}, f32[1,216]{1,0:T(1,128)}, u32[]{:S(2)}) copy-start(f32[1,216]{1,0:T(1,128)} %get-tuple-element.129) | copy-start | bytes 2596
  100.9 38.2 %copy-start.54 = (f32[1,216]{1,0:T(1,128)S(1)}, f32[1,216]{1,0:T(1,128)}, u32[]{:S(2)}) copy-start(f32[1,216]{1,0:T(1,128)} %get-tuple-element.132) | copy-start | bytes 2596
  102.2 79.8 %all-reduce.12.cloned.1.call-start = ((), (), s32[]{:S(2)}) async-start(), calls=%async_computation.7 | async-start | bytes 1638400 | tf_op jit(solution)/shard_map/psum | solution.py:206
  102.4 39.5 %copy-start.62 = (f32[4]{0:T(128)}, f32[4]{0:T(128)S(1)}, u32[]{:S(2)}) copy-start(f32[4]{0:T(128)S(1)} %compare_convert_fusion.1) | copy-start | bytes 52
  103.9 38.0 %copy-start.21 = (bf16[216,216,1]{1,0,2:T(8,128)(2,1)}, bf16[216,216,1]{1,0,2:T(8,128)(2,1)S(1)}, u32[]{:S(2)}) copy-start(bf16[216,216,1]{1,0,2:T(8,128)(2,1)S(1)} %reshape.190) | copy-start | bytes 279940
  104.0 38.0 %copy-start.48 = (f32[216]{0:T(256)}, f32[216]{0:T(256)S(1)}, u32[]{:S(2)}) copy-start(f32[216]{0:T(256)S(1)} %compare_convert_fusion.2) | copy-start | bytes 2596
  146.9 70.1 %all-reduce.10.cloned.1.call-start = ((), (), s32[]{:S(2)}) async-start(), calls=%async_computation.6 | async-start | bytes 819200 | tf_op jit(solution)/shard_map/psum | solution.py:189
  150.2 66.8 %copy-start.45 = (f32[1,216]{1,0:T(1,128)S(1)}, f32[1,216]{1,0:T(1,128)}, u32[]{:S(2)}) copy-start(f32[1,216]{1,0:T(1,128)} %get-tuple-element.129) | copy-start | bytes 2596
  155.6 64.2 %copy-start.67 = (f32[3]{0:T(128)S(1)}, f32[3]{0:T(128)}, u32[]{:S(2)}) copy-start(f32[3]{0:T(128)} %copy-done.66) | copy-start | bytes 40
  156.8 60.2 %copy-start.26 = (f32[9,864]{1,0:T(8,128)}, f32[9,864]{1,0:T(8,128)S(1)}, u32[]{:S(2)}) copy-start(f32[9,864]{1,0:T(8,128)S(1)} %dynamic_update_slice.3) | copy-start | bytes 93316
  223.1 20.5 %all-to-all-start.2 = ((bf16[4,3,196,196]{3,0,1,2:T(4,128)(2,1)}), bf16[4,3,196,196]{3,0,1,2:T(4,128)(2,1)}, u32[]{:S(2)}, u32[]{:S(2)}) async-start(bf16[4,3,196,196]{3,0,1,2:T(4,128)(2,1)} %copy.239), calls=%async_computation.2 | async-start | bytes 2408448 | tf_op jit(solution)/shard_map/all_to_all | solution.py:236
  256.4 20.5 %all-to-all-start.3 = ((bf16[4,12,49,196]{3,0,2,1:T(4,128)(2,1)}), bf16[4,12,49,196]{3,0,2,1:T(4,128)(2,1)}, u32[]{:S(2)}, u32[]{:S(2)}) async-start(bf16[4,12,49,196]{3,0,2,1:T(4,128)(2,1)} %copy.245), calls=%async_computation.3 | async-start | bytes 2408448 | tf_op jit(solution)/shard_map/all_to_all | solution.py:240
  260.7 55.2 %all-reduce.14.cloned.1.call-start = ((), (), s32[]{:S(2)}) async-start(), calls=%async_computation.8 | async-start | bytes 1638400 | tf_op jit(solution)/shard_map/psum | solution.py:260
  281.0 101.6 %reduce-scatter.2.cloned.1.call-start = ((), (), s32[]{:S(2)}) async-start(), calls=%async_computation.9 | async-start | bytes 1032192 | tf_op jit(solution)/shard_map/reduce_scatter | solution.py:296
  283.2 37.5 %copy-start.57 = (f32[216]{0:T(256)S(1)}, f32[216]{0:T(256)}, u32[]{:S(2)}) copy-start(f32[216]{0:T(256)} %get-tuple-element.84) | copy-start | bytes 2596
  283.2 78.5 %copy-start.34 = (f32[2,12,12]{2,0,1:T(2,128)S(1)}, f32[2,12,12]{2,0,1:T(2,128)}, u32[]{:S(2)}) copy-start(f32[2,12,12]{2,0,1:T(2,128)} %param.30) | copy-start | bytes 3460
  283.2 78.5 %copy-start.46 = (f32[2,12,12]{2,0,1:T(2,128)S(1)}, f32[2,12,12]{2,0,1:T(2,128)}, u32[]{:S(2)}) copy-start(f32[2,12,12]{2,0,1:T(2,128)} %param.31) | copy-start | bytes 3460
  283.2 78.5 %copy-start.47 = (f32[2,12,12]{2,0,1:T(2,128)S(1)}, f32[2,12,12]{2,0,1:T(2,128)}, u32[]{:S(2)}) copy-start(f32[2,12,12]{2,0,1:T(2,128)} %param.32) | copy-start | bytes 3460
  284.1 79.4 %copy-start.43 = (f32[4,216]{1,0:T(4,128)S(1)}, f32[4,216]{1,0:T(4,128)}, u32[]{:S(2)}) copy-start(f32[4,216]{1,0:T(4,128)} %param.27) | copy-start | bytes 10372
  284.1 79.4 %copy-start.55 = (f32[4,216]{1,0:T(4,128)S(1)}, f32[4,216]{1,0:T(4,128)}, u32[]{:S(2)}) copy-start(f32[4,216]{1,0:T(4,128)} %param.28) | copy-start | bytes 10372
  284.1 79.4 %copy-start.56 = (f32[4,216]{1,0:T(4,128)S(1)}, f32[4,216]{1,0:T(4,128)}, u32[]{:S(2)}) copy-start(f32[4,216]{1,0:T(4,128)} %param.29) | copy-start | bytes 10372
  284.1 80.0 %copy-start.36 = (f32[9,216]{1,0:T(8,128)S(1)}, f32[9,216]{1,0:T(8,128)}, u32[]{:S(2)}) copy-start(f32[9,216]{1,0:T(8,128)} %param.33) | copy-start | bytes 23332
  284.1 80.0 %copy-start.41 = (f32[9,216]{1,0:T(8,128)S(1)}, f32[9,216]{1,0:T(8,128)}, u32[]{:S(2)}) copy-start(f32[9,216]{1,0:T(8,128)} %param.34) | copy-start | bytes 23332
  284.2 80.0 %copy-start.42 = (f32[9,216]{1,0:T(8,128)S(1)}, f32[9,216]{1,0:T(8,128)}, u32[]{:S(2)}) copy-start(f32[9,216]{1,0:T(8,128)} %param.35) | copy-start | bytes 23332
  284.2 98.4 %copy-start.22 = (f32[2,54,216]{2,0,1:T(2,128)S(1)}, f32[2,54,216]{2,0,1:T(2,128)}, u32[]{:S(2)}) copy-start(f32[2,54,216]{2,0,1:T(2,128)} %param.24) | copy-start | bytes 279940
  284.2 98.4 %copy-start.31 = (f32[2,54,216]{2,0,1:T(2,128)S(1)}, f32[2,54,216]{2,0,1:T(2,128)}, u32[]{:S(2)}) copy-start(f32[2,54,216]{2,0,1:T(2,128)} %param.25) | copy-start | bytes 279940
  284.2 98.3 %copy-start.32 = (f32[2,54,216]{2,0,1:T(2,128)S(1)}, f32[2,54,216]{2,0,1:T(2,128)}, u32[]{:S(2)}) copy-start(f32[2,54,216]{2,0,1:T(2,128)} %param.26) | copy-start | bytes 279940
  (46 other events, 453.8 us)
Sparse Core Ops, SparseCore 0:
  102.3 34.9 all-reduce.7
  147.0 34.9 all-reduce.11
  184.4 32.5 all-reduce.9
  281.1 34.8 all-reduce.13
  319.5 63.0 reduce-scatter.1
where the time goes:
time: 394 us; the launch traced here: 393 us
  waiting for transfers between devices  186 us (47%)
  blocking collectives  73.8 us (19%)
  matrix products  40.3 us (10%)
  local copies, waits for them, and re-layouts  34.1 us (9%)
  other arithmetic  25.5 us (6%)
  between operations  17 us (4%)
  starting transfers between devices  16.5 us (4%)
    psum x1, blocking collectives, local(): lax.psum((norm_part, talk_part, conv_wide), ('dp', 'head'))  41 us
    psum x1, waiting for transfers between devices, local(): middle = token_values + lax.psum(attn_part, 'head')  33.3 us
    all_gather x1, blocking collectives, local(): lax.all_gather(master.astype(jnp.bfloat16), 'dp', axis=0, tiled=True)  32.9 us
    psum x1, waiting for transfers between devices, local(): lax.psum(down_part.astype(jnp.bfloat16), 'head').astype(jnp.float32)  32.6 us
    psum x1, waiting for transfers between devices, local(): grad_normed_one = lax.psum(grad_one_part, 'head')  31.7 us
    psum x1, waiting for transfers between devices, local(): grad_normed_two = lax.psum(grad_two_part, 'head')  25.2 us
    reduce_scatter x1, waiting for transfers between devices, local(): lax.psum_scatter(spread_grads, 'dp', scatter_dimension=0, tiled=True)  17.6 us
    all_to_all x1, waiting for transfers between devices, local(): lax.all_to_all(scores, 'head', split_axis=2, concat_axis=1, tiled=True)  16.1 us
  transfers between devices with their start and end apart: 9, of which 9 were waited for; matrix products, arithmetic and copies ran while one was open for 10% of the time, Pallas kernels for 0%

commit v1 on v0

--- a/solution.py
+++ b/solution.py
@@ -129,7 +129,15 @@
     per_head = block_rows // HD
     hidden_local = 4 * block_rows
     scale_factor = HD ** (-0.5)
-    every_slot = lax.all_gather(master.astype(jnp.bfloat16), "dp", axis=0, tiled=True)
+    x = master.astype(jnp.bfloat16)
+    ways, here, turn = (lax.axis_size("dp"), lax.axis_index("dp"), x.shape[0])
+    line, have = (x, 1)
+    while have < ways:
+        line = jnp.concatenate(
+            [line, lax.ppermute(line, "dp", [(d, (d - have) % ways) for d in range(ways)])], axis=0
+        )
+        have = 2 * have
+    every_slot = jnp.roll(line, here * turn, axis=0)
     blocks = jnp.take(every_slot, block_slot, axis=0)
     w_qkv = blocks[0:3].reshape(3 * block_rows, model_width)
     w_out = blocks[3]

time: 394 us -> 380 us (0.964)
  blocking collectives: 73.8 us -> 41 us
  waiting for transfers between devices: 186 us -> 199 us
  starting transfers between devices: 16.5 us -> 23.1 us
    all_gather x1 -> x0, blocking collectives: 32.9 us -> none  [local(): lax.all_gather(master.astype(jnp.bfloat16), 'dp', axis=0, tiled=True)]
    ppermute x0 -> x3, waiting for transfers between devices: none -> 15.6 us  [local(): lax.ppermute(line, 'dp', [(d, (d - have) % ways) for d in range(ways)])]
    ppermute x0 -> x3, starting transfers between devices: none -> 6.6 us  [local(): lax.ppermute(line, 'dp', [(d, (d - have) % ways) for d in range(ways)])]
    unnamed x148 -> x167, local copies, waits for them, and re-layouts: 11.6 us -> 12.1 us
  transfers between devices with their start and end apart: 9 -> 12, of which waited for: 9 -> 11; matrix products, arithmetic and copies ran while one was open for 10% -> 12% of each run, Pallas kernels for 0% -> 0%
where the time goes in v1:
time: 380 us; the launch traced here: 379 us
  waiting for transfers between devices  199 us (52%)
  blocking collectives  41 us (11%)
  matrix products  39 us (10%)
  local copies, waits for them, and re-layouts  34.7 us (9%)
  other arithmetic  25.1 us (7%)
  starting transfers between devices  23.1 us (6%)
  between operations  17.1 us (5%)
    psum x1, blocking collectives, local(): lax.psum((norm_part, talk_part, conv_wide), ('dp', 'head'))  41 us
    psum x1, waiting for transfers between devices, local(): lax.psum(down_part.astype(jnp.bfloat16), 'head').astype(jnp.float32)  32.6 us
    psum x1, waiting for transfers between devices, local(): grad_normed_one = lax.psum(grad_one_part, 'head')  31.7 us
    psum x1, waiting for transfers between devices, local(): middle = token_values + lax.psum(attn_part, 'head')  31.2 us
    psum x1, waiting for transfers between devices, local(): grad_normed_two = lax.psum(grad_two_part, 'head')  25.2 us
    reduce_scatter x1, waiting for transfers between devices, local(): lax.psum_scatter(spread_grads, 'dp', scatter_dimension=0, tiled=True)  17.7 us
    all_to_all x1, waiting for transfers between devices, local(): lax.all_to_all(scores, 'head', split_axis=2, concat_axis=1, tiled=True)  16.1 us
    ppermute x3, waiting for transfers between devices, local(): lax.ppermute(line, 'dp', [(d, (d - have) % ways) for d in range(ways)])  15.6 us
  transfers between devices with their start and end apart: 12, of which 11 were waited for; matrix products, arithmetic and copies ran while one was open for 12% of the time, Pallas kernels for 0%

profile of v1, /device:TPU:0, one launch (start us, length us, event | category | flops | bytes accessed | tf_op | source)
XLA Modules:
  0.0 379.3 jit_solution(4645088166002255049)
XLA Ops:
  8.2 6.0 %collective-permute-start = (bf16[2,54,216]{2,1,0:T(8,128)(2,1)S(1)}, bf16[2,54,216]{2,1,0:T(8,128)(2,1)S(1)}, u32[]{:S(2)}, u32[]{:S(2)}) collective-permute-start(bf16[2,54,216]{2,1,0:T(8,128)(2,1)S(1)} %get-tuple-element.98), channel_id=1, source_target_pairs={{0,28},{4,0},{8,4},{12,8},{16,12},{20,16},{24,20},{28,24},{1,29},{... | collective-permute-start | bytes 139976 | tf_op jit(solution)/shard_map/ppermute | solution.py:137
  20.1 4.3 %collective-permute-done.1 = bf16[4,54,216]{2,1,0:T(8,128)(2,1)S(1)} collective-permute-done((bf16[4,54,216]{2,1,0:T(8,128)(2,1)S(1)}, bf16[4,54,216]{2,1,0:T(8,128)(2,1)S(1)}, u32[]{:S(2)}, u32[]{:S(2)}) %collective-permute-start.1) | collective-permute-done | bytes 93344 | tf_op jit(solution)/shard_map/ppermute | solution.py:137
  24.6 11.3 %collective-permute-done.2 = bf16[8,54,216]{2,1,0:T(8,128)(2,1)S(1)} collective-permute-done((bf16[8,54,216]{2,1,0:T(8,128)(2,1)S(1)}, bf16[8,54,216]{2,1,0:T(8,128)(2,1)S(1)}, u32[]{:S(2)}, u32[]{:S(2)}) %collective-permute-start.2) | collective-permute-done | bytes 186656 | tf_op jit(solution)/shard_map/ppermute | solution.py:137
  39.6 3.5 all-to-all-start
  43.2 16.1 %all-to-all-done = bf16[4,3,196,196]{3,0,1,2:T(4,128)(2,1)S(1)} async-done(((bf16[4,3,196,196]{3,0,1,2:T(4,128)(2,1)}), bf16[4,3,196,196]{3,0,1,2:T(4,128)(2,1)S(1)}, u32[]{:S(2)}, u32[]{:S(2)}) %all-to-all-start) | async-done | bytes 922016 | tf_op jit(solution)/shard_map/all_to_all | solution.py:165
  59.7 2.0 bitcast_reduce_fusion
  62.9 3.7 fusion.13
  68.3 3.5 all-to-all-start.1
  75.6 12.4 %all-to-all-done.1 = bf16[4,12,49,196]{3,0,2,1:T(4,128)(2,1)S(1)} async-done(((bf16[4,12,49,196]{3,0,2,1:T(4,128)(2,1)}), bf16[4,12,49,196]{3,0,2,1:T(4,128)(2,1)S(1)}, u32[]{:S(2)}, u32[]{:S(2)}) %all-to-all-start.1) | async-done | bytes 922016 | tf_op jit(solution)/shard_map/all_to_all | solution.py:167
  92.4 31.2 %all-reduce.8.cloned.1.call-done = f32[4,196,216]{2,1,0:T(8,128)} async-done(((f32[4,196,216]{2,1,0:T(8,128)}), f32[4,196,216]{2,1,0:T(8,128)}) %all-reduce.8.cloned.1.call-update) | async-done | bytes 677392 | tf_op jit(solution)/shard_map/psum | solution.py:188
  129.2 1.7 multiply_reduce_fusion
  133.3 2.2 fusion.80
  139.9 2.0 convolution_convert_fusion.3
  143.2 25.2 %all-reduce.12.cloned.1.call-done = f32[4,196,216]{2,1,0:T(8,128)} async-done(((f32[4,196,216]{2,1,0:T(8,128)}), f32[4,196,216]{2,1,0:T(8,128)}) %all-reduce.12.cloned.1.call-update) | async-done | bytes 677392 | tf_op jit(solution)/shard_map/psum | solution.py:214
  168.4 2.4 multiply_reduce_fusion.9
  170.7 32.6 %all-reduce.10.cloned.1.call-done = bf16[4,196,216]{2,1,0:T(8,128)(2,1)} async-done(((bf16[4,196,216]{2,1,0:T(8,128)(2,1)}), bf16[4,196,216]{2,1,0:T(8,128)(2,1)}) %all-reduce.10.cloned.1.call-update) | async-done | bytes 338704 | tf_op jit(solution)/shard_map/psum | solution.py:197
  203.4 2.8 multiply_add_fusion.1
  209.5 4.5 %all-to-all-start.2 = ((bf16[4,3,196,196]{3,0,1,2:T(4,128)(2,1)}), bf16[4,3,196,196]{3,0,1,2:T(4,128)(2,1)}, u32[]{:S(2)}, u32[]{:S(2)}) async-start(bf16[4,3,196,196]{3,0,1,2:T(4,128)(2,1)} %copy.163), calls=%async_computation.2 | async-start | bytes 2408448 | tf_op jit(solution)/shard_map/all_to_all | solution.py:244
  215.5 2.4 convolution_bitcast_fusion
  217.9 2.4 copy.200
  220.9 9.1 %all-to-all-done.2 = bf16[4,3,196,196]{3,0,1,2:T(4,128)(2,1)} async-done(((bf16[4,3,196,196]{3,0,1,2:T(4,128)(2,1)}), bf16[4,3,196,196]{3,0,1,2:T(4,128)(2,1)}, u32[]{:S(2)}, u32[]{:S(2)}) %all-to-all-start.2) | async-done | bytes 922016 | tf_op jit(solution)/shard_map/all_to_all | solution.py:244
  231.7 4.7 %fusion = (f32[4,12,49]{1,2,0:T(8,128)S(1)}, f32[4,49,196,12]{2,3,1,0:T(8,128)S(1)}) fusion(f32[4,12,49]{1,2,0:T(8,128)S(1)} %copy-done.27, f32[4,12,49]{1,2,0:T(8,128)S(1)} %copy-done.18, f32[4,49,196,12]{2,3,1,0:T(8,128)} %copy-done, f32[2,12,12]{2,1,0:T(8,128)S(1)} %copy-done.37, bf16[4,12,49,196]{3,0,2,1:T(4,128)(2,1)S(1)} %bitcast.228), kind=kOutput, calls=%fused_computation.4 | convolution fusion | flops 68224464 | bytes 5139136 | tf_op jit(solution)/shard_map/jm,gjqk->gmqk/dot_general | solution.py:79
  236.5 4.7 %fusion.14 = bf16[4,12,49,196]{3,1,2,0:T(8,128)(2,1)S(1)} fusion(f32[4,49,196,12]{2,3,1,0:T(8,128)S(1)} %get-tuple-element.123, f32[4,12,49]{1,2,0:T(8,128)S(1)} %get-tuple-element.122, f32[2,12,12]{2,1,0:T(8,128)S(1)} %copy-done.37, f32[4,49,196,12]{2,3,1,0:T(8,128)S(1)} %copy-done.1, f32[4,12,49]{1,2,0:T(8,128)S(1)} %copy-done.27, ...), kind=kOutput, calls=%fused_computation.24 | convolution fusion | flops 68687808 | bytes 7696768 | tf_op jit(solution)/shard_map/mn,gmqk->gnqk/dot_general | solution.py:85
  242.8 4.3 %all-to-all-start.3 = ((bf16[4,12,49,196]{3,0,2,1:T(4,128)(2,1)}), bf16[4,12,49,196]{3,0,2,1:T(4,128)(2,1)}, u32[]{:S(2)}, u32[]{:S(2)}) async-start(bf16[4,12,49,196]{3,0,2,1:T(4,128)(2,1)} %copy.169), calls=%async_computation.3 | async-start | bytes 2408448 | tf_op jit(solution)/shard_map/all_to_all | solution.py:248
  247.2 5.7 %fusion.27 = f32[1,12,12]{2,1,0:T(8,128)S(1)} fusion(bf16[4,12,49,196]{3,0,2,1:T(4,128)(2,1)S(1)} %bitcast.211, f32[4,49,196,12]{2,3,1,0:T(8,128)} %copy-done.74, f32[4,12,49]{1,2,0:T(8,128)S(1)} %get-tuple-element.122, f32[4,49,196,12]{2,3,1,0:T(8,128)} %copy-done, f32[4,12,49]{1,2,0:T(8,128)S(1)} %copy-done.27, f32[4,12,49]{1,2,0:T(8,128)S(1)} %copy-done.18), kind=kOutput, calls=%fused_computation.50 | convolution fusion | flops 68226816 | bytes 4638720 | tf_op jit(solution)/shard_map/gmqk,gnqk->mn/dot_general | solution.py:82
  252.9 2.8 fusion.32
  255.7 7.6 %all-to-all-done.3 = bf16[4,12,49,196]{3,0,2,1:T(4,128)(2,1)} async-done(((bf16[4,12,49,196]{3,0,2,1:T(4,128)(2,1)}), bf16[4,12,49,196]{3,0,2,1:T(4,128)(2,1)}, u32[]{:S(2)}, u32[]{:S(2)}) %all-to-all-start.3) | async-done | bytes 922016 | tf_op jit(solution)/shard_map/all_to_all | solution.py:248
  263.3 1.7 copy.170
  270.6 31.7 %all-reduce.14.cloned.1.call-done = f32[4,196,216]{2,1,0:T(8,128)} async-done(((f32[4,196,216]{2,1,0:T(8,128)}), f32[4,196,216]{2,1,0:T(8,128)}) %all-reduce.14.cloned.1.call-update) | async-done | bytes 677392 | tf_op jit(solution)/shard_map/psum | solution.py:268
  302.3 1.8 fusion.68
  307.1 41.0 %all-reduce.2 = (f32[4,216]{1,0:T(4,128)S(1)}, f32[2,12,12]{2,1,0:T(8,128)S(1)}, f32[9,864]{1,0:T(8,128)S(1)}) all-reduce(f32[4,216]{1,0:T(4,128)S(1)} %pad_maximum_fusion.5, f32[2,12,12]{2,1,0:T(8,128)S(1)} %pad_maximum_fusion.4, f32[9,864]{1,0:T(8,128)S(1)} %copy-done.25), channel_id=1, replica_groups=mesh['dp'=8,'head'=4] {'dp','head'}, use_global_device_ids=true, to_apply=%region_21.22 | all-reduce | flops 8928 | bytes 71424 | tf_op jit(solution)/shard_map/psum | solution.py:287
  351.3 17.7 %reduce-scatter.2.cloned.1.call-done = f32[2,54,216]{2,1,0:T(8,128)} async-done(((f32[16,54,216]{2,1,0:T(8,128)}), f32[2,54,216]{2,1,0:T(8,128)}) %reduce-scatter.2.cloned.1.call-update) | async-done | bytes 93328 | tf_op jit(solution)/shard_map/reduce_scatter | solution.py:304
  (267 shorter events, 57.1 us)
Async XLA Ops:
  8.2 11.4 %collective-permute-start = (bf16[2,54,216]{2,1,0:T(8,128)(2,1)S(1)}, bf16[2,54,216]{2,1,0:T(8,128)(2,1)S(1)}, u32[]{:S(2)}, u32[]{:S(2)}) collective-permute-start(bf16[2,54,216]{2,1,0:T(8,128)(2,1)S(1)} %get-tuple-element.98), channel_id=1, source_target_pairs={{0,28},{4,0},{8,4},{12,8},{16,12},{20,16},{24,20},{28,24},{1,29},{... | collective-permute-start | bytes 139976 | tf_op jit(solution)/shard_map/ppermute | solution.py:137
  19.6 4.8 %collective-permute-start.1 = (bf16[4,54,216]{2,1,0:T(8,128)(2,1)S(1)}, bf16[4,54,216]{2,1,0:T(8,128)(2,1)S(1)}, u32[]{:S(2)}, u32[]{:S(2)}) collective-permute-start(bf16[4,54,216]{2,1,0:T(8,128)(2,1)S(1)} %pad_maximum_fusion.3), channel_id=1, source_target_pairs={{0,24},{4,28},{8,0},{12,4},{16,8},{20,12},{24,16},{28,20},{1,25},{... | collective-permute-start | bytes 279944 | tf_op jit(solution)/shard_map/ppermute | solution.py:137
  24.5 11.4 %collective-permute-start.2 = (bf16[8,54,216]{2,1,0:T(8,128)(2,1)S(1)}, bf16[8,54,216]{2,1,0:T(8,128)(2,1)S(1)}, u32[]{:S(2)}, u32[]{:S(2)}) collective-permute-start(bf16[8,54,216]{2,1,0:T(8,128)(2,1)S(1)} %pad_maximum_fusion.2), channel_id=1, source_target_pairs={{0,16},{4,20},{8,24},{12,28},{16,0},{20,4},{24,8},{28,12},{1,17},{... | collective-permute-start | bytes 559880 | tf_op jit(solution)/shard_map/ppermute | solution.py:137
  37.6 50.8 %copy-start.16 = (bf16[4,196,1,3,18]{1,0,4,3,2:T(4,128)(2,1)}, bf16[4,196,1,3,18]{1,0,4,3,2:T(4,128)(2,1)S(1)}, u32[]{:S(2)}) copy-start(bf16[4,196,1,3,18]{1,0,4,3,2:T(4,128)(2,1)S(1)} %get-tuple-element.104) | copy-start | bytes 254020
  39.6 19.6 %all-to-all-start = ((bf16[4,3,196,196]{3,0,1,2:T(4,128)(2,1)}), bf16[4,3,196,196]{3,0,1,2:T(4,128)(2,1)S(1)}, u32[]{:S(2)}, u32[]{:S(2)}) async-start(bf16[4,3,196,196]{3,0,1,2:T(4,128)(2,1)} %copy.139), calls=%async_computation | async-start | bytes 2408448 | tf_op jit(solution)/shard_map/all_to_all | solution.py:165
  68.3 19.6 %all-to-all-start.1 = ((bf16[4,12,49,196]{3,0,2,1:T(4,128)(2,1)}), bf16[4,12,49,196]{3,0,2,1:T(4,128)(2,1)S(1)}, u32[]{:S(2)}, u32[]{:S(2)}) async-start(bf16[4,12,49,196]{3,0,2,1:T(4,128)(2,1)} %copy.145), calls=%async_computation.1 | async-start | bytes 2408448 | tf_op jit(solution)/shard_map/all_to_all | solution.py:167
  71.9 51.7 %all-reduce.8.cloned.1.call-start = ((), (), s32[]{:S(2)}) async-start(), calls=%async_computation.5 | async-start | bytes 1638400 | tf_op jit(solution)/shard_map/psum | solution.py:188
  91.2 77.2 %all-reduce.12.cloned.1.call-start = ((), (), s32[]{:S(2)}) async-start(), calls=%async_computation.7 | async-start | bytes 1638400 | tf_op jit(solution)/shard_map/psum | solution.py:214
  91.4 36.9 %copy-start.68 = (f32[4]{0:T(128)}, f32[4]{0:T(128)S(1)}, u32[]{:S(2)}) copy-start(f32[4]{0:T(128)S(1)} %compare_convert_fusion.1) | copy-start | bytes 52
  133.2 70.1 %all-reduce.10.cloned.1.call-start = ((), (), s32[]{:S(2)}) async-start(), calls=%async_computation.6 | async-start | bytes 819200 | tf_op jit(solution)/shard_map/psum | solution.py:197
  136.6 66.8 %copy-start.42 = (f32[1,216]{1,0:T(1,128)S(1)}, f32[1,216]{1,0:T(1,128)}, u32[]{:S(2)}) copy-start(f32[1,216]{1,0:T(1,128)} %get-tuple-element.116) | copy-start | bytes 2596
  142.0 64.2 %copy-start.73 = (f32[3]{0:T(128)S(1)}, f32[3]{0:T(128)}, u32[]{:S(2)}) copy-start(f32[3]{0:T(128)} %copy-done.72) | copy-start | bytes 40
  143.2 60.2 %copy-start.24 = (f32[9,864]{1,0:T(8,128)}, f32[9,864]{1,0:T(8,128)S(1)}, u32[]{:S(2)}) copy-start(f32[9,864]{1,0:T(8,128)S(1)} %dynamic_update_slice.3) | copy-start | bytes 93316
  209.5 20.5 %all-to-all-start.2 = ((bf16[4,3,196,196]{3,0,1,2:T(4,128)(2,1)}), bf16[4,3,196,196]{3,0,1,2:T(4,128)(2,1)}, u32[]{:S(2)}, u32[]{:S(2)}) async-start(bf16[4,3,196,196]{3,0,1,2:T(4,128)(2,1)} %copy.163), calls=%async_computation.2 | async-start | bytes 2408448 | tf_op jit(solution)/shard_map/all_to_all | solution.py:244
  242.8 20.5 %all-to-all-start.3 = ((bf16[4,12,49,196]{3,0,2,1:T(4,128)(2,1)}), bf16[4,12,49,196]{3,0,2,1:T(4,128)(2,1)}, u32[]{:S(2)}, u32[]{:S(2)}) async-start(bf16[4,12,49,196]{3,0,2,1:T(4,128)(2,1)} %copy.169), calls=%async_computation.3 | async-start | bytes 2408448 | tf_op jit(solution)/shard_map/all_to_all | solution.py:248
  247.1 55.2 %all-reduce.14.cloned.1.call-start = ((), (), s32[]{:S(2)}) async-start(), calls=%async_computation.8 | async-start | bytes 1638400 | tf_op jit(solution)/shard_map/psum | solution.py:268
  267.4 101.6 %reduce-scatter.2.cloned.1.call-start = ((), (), s32[]{:S(2)}) async-start(), calls=%async_computation.9 | async-start | bytes 1032192 | tf_op jit(solution)/shard_map/reduce_scatter | solution.py:304
  269.5 37.5 %copy-start.63 = (f32[216]{0:T(256)S(1)}, f32[216]{0:T(256)}, u32[]{:S(2)}) copy-start(f32[216]{0:T(256)} %get-tuple-element.69) | copy-start | bytes 2596
  269.5 37.5 %copy-start.64 = (f32[216]{0:T(256)S(1)}, f32[216]{0:T(256)}, u32[]{:S(2)}) copy-start(f32[216]{0:T(256)} %get-tuple-element.76) | copy-start | bytes 2596
  269.6 37.5 %copy-start.25 = (f32[9,864]{1,0:T(8,128)S(1)}, f32[9,864]{1,0:T(8,128)}, u32[]{:S(2)}) copy-start(f32[9,864]{1,0:T(8,128)} %copy-done.24) | copy-start | bytes 93316
  269.6 78.5 %copy-start.31 = (f32[2,12,12]{2,0,1:T(2,128)S(1)}, f32[2,12,12]{2,0,1:T(2,128)}, u32[]{:S(2)}) copy-start(f32[2,12,12]{2,0,1:T(2,128)} %param.30) | copy-start | bytes 3460
  269.6 78.5 %copy-start.43 = (f32[2,12,12]{2,0,1:T(2,128)S(1)}, f32[2,12,12]{2,0,1:T(2,128)}, u32[]{:S(2)}) copy-start(f32[2,12,12]{2,0,1:T(2,128)} %param.31) | copy-start | bytes 3460
  269.6 78.5 %copy-start.44 = (f32[2,12,12]{2,0,1:T(2,128)S(1)}, f32[2,12,12]{2,0,1:T(2,128)}, u32[]{:S(2)}) copy-start(f32[2,12,12]{2,0,1:T(2,128)} %param.32) | copy-start | bytes 3460
  270.5 79.5 %copy-start.40 = (f32[4,216]{1,0:T(4,128)S(1)}, f32[4,216]{1,0:T(4,128)}, u32[]{:S(2)}) copy-start(f32[4,216]{1,0:T(4,128)} %param.27) | copy-start | bytes 10372
  270.5 79.4 %copy-start.61 = (f32[4,216]{1,0:T(4,128)S(1)}, f32[4,216]{1,0:T(4,128)}, u32[]{:S(2)}) copy-start(f32[4,216]{1,0:T(4,128)} %param.28) | copy-start | bytes 10372
  270.5 79.4 %copy-start.62 = (f32[4,216]{1,0:T(4,128)S(1)}, f32[4,216]{1,0:T(4,128)}, u32[]{:S(2)}) copy-start(f32[4,216]{1,0:T(4,128)} %param.29) | copy-start | bytes 10372
  270.5 80.0 %copy-start.33 = (f32[9,216]{1,0:T(8,128)S(1)}, f32[9,216]{1,0:T(8,128)}, u32[]{:S(2)}) copy-start(f32[9,216]{1,0:T(8,128)} %param.33) | copy-start | bytes 23332
  270.6 80.0 %copy-start.38 = (f32[9,216]{1,0:T(8,128)S(1)}, f32[9,216]{1,0:T(8,128)}, u32[]{:S(2)}) copy-start(f32[9,216]{1,0:T(8,128)} %param.34) | copy-start | bytes 23332
  270.6 80.0 %copy-start.39 = (f32[9,216]{1,0:T(8,128)S(1)}, f32[9,216]{1,0:T(8,128)}, u32[]{:S(2)}) copy-start(f32[9,216]{1,0:T(8,128)} %param.35) | copy-start | bytes 23332
  270.6 98.4 %copy-start.19 = (f32[2,54,216]{2,0,1:T(2,128)S(1)}, f32[2,54,216]{2,0,1:T(2,128)}, u32[]{:S(2)}) copy-start(f32[2,54,216]{2,0,1:T(2,128)} %param.24) | copy-start | bytes 279940
  270.6 98.4 %copy-start.28 = (f32[2,54,216]{2,0,1:T(2,128)S(1)}, f32[2,54,216]{2,0,1:T(2,128)}, u32[]{:S(2)}) copy-start(f32[2,54,216]{2,0,1:T(2,128)} %param.25) | copy-start | bytes 279940
  270.6 98.4 %copy-start.29 = (f32[2,54,216]{2,0,1:T(2,128)S(1)}, f32[2,54,216]{2,0,1:T(2,128)}, u32[]{:S(2)}) copy-start(f32[2,54,216]{2,0,1:T(2,128)} %param.26) | copy-start | bytes 279940
  (55 other events, 809.5 us)
Sparse Core Ops, SparseCore 0:
  91.3 32.2 all-reduce.7
  133.4 34.9 all-reduce.11
  170.7 32.5 all-reduce.9
  267.5 34.8 all-reduce.13
  305.9 63.0 reduce-scatter.1
